TPU v7x, 32 devices: a whole 2x2x4 slice. The times are simulated.
32 devices in a mesh: gx: 8 (over z, core), gy: 4 (over y, x).
Axes of the slice: x: 2, y: 2, z: 4, core: 2. Of those that a mesh axis runs over, the one named last changes fastest.
Arguments:
- suction_potential: float32 [64, 32, 128], P('gx', 'gy'), may hold values from -3 to 0.3
- ground_warmth: float32 [64, 32, 128], P('gx', 'gy'), may hold values from -4 to 4
- ground_category: int32 [64, 32, 128], P('gx', 'gy'), may hold values from 0 to 11
- icebound_flag: int32 [64, 32, 128], P('gx', 'gy'), may hold values 0 or 1
- ground_wetted_permeability: float32 [12], replicated, may hold values from 0.02 to 0.15
- ground_falloff_exponent: float32 [12], replicated, may hold values from 0.3 to 1.5
- camera_skew_per_plane: float32 [4], replicated, may hold values from -1 to 1
- hue_gradient_steepness: float32 [3], replicated, may hold values from 4 to 16
- hue_gradient_middles: float32 [3], replicated, may hold values from 0.1 to 0.4
- camera_distance_ordering: int32 [4, 4], replicated, may hold values from 0 to 3, as said below
Outputs:
- head_out: float32 [64, 32, 128], P('gx', 'gy')
- temp_out: float32 [64, 32, 128], P('gx', 'gy')
- image: float32 [4, 4, 64, 128], P(None, None, 'gx', 'gy')
Inputs may be any that keep to these rules, and one draw needn't show every extreme that they name: Each row of camera_distance_ordering names every slab 0 to 3 once.
All inputs are finite; a program needn't handle non-finite values. No bound on the sum of `icebound_flag` on one device may be relied on, other than what follows from the above.
Results may differ from a plain program's by a relative error of at most 0.0003.
Values sent between devices are 32-bit elements; how exact they have to be, the bound alone decides.
No kernel may reach another device: no remote copies, remote signals or barrier semaphores. Data moves between devices by JAX's collectives and lax.ppermute only.
A program may use at most 64 MiB of HBM per device.

v0:
```python
import jax
import jax.numpy as jnp
from jax import lax
from jax.sharding import PartitionSpec as P

STEPS = 2
IMPEDANCE = 4.0
DIFFUSE = 0.12


def with_halo(x, sides, width):
    for axis, dim in sides:
        count, length = (lax.axis_size(axis), x.shape[dim])
        up = [(i, (i + 1) % count) for i in range(count - 1)]
        down = [(j, i) for i, j in up]
        last = lax.slice_in_dim(x, length - width, length, axis=dim)
        first = lax.slice_in_dim(x, 0, width, axis=dim)
        before = lax.ppermute(last, axis, up)
        after = lax.ppermute(first, axis, down)
        x = jnp.concatenate([before, x, after], axis=dim)
    return x


def voxel_index_map(ground_category, table):
    total = jnp.zeros(ground_category.shape, jnp.float32)
    for number in range(table.shape[0]):
        total = total + jnp.where(ground_category == number, table[number], jnp.float32(0.0))
    return total


def advance(evolving_arrays, first_row, first_col, rows_all, cols_all):
    suction_potential, temp, conduct_sat, alpha, ice = evolving_arrays
    conduct = (
        conduct_sat
        * jnp.exp(alpha * jnp.minimum(suction_potential, 0.0))
        * jnp.exp(-IMPEDANCE * ice * jax.nn.sigmoid(-2.0 * temp))
    )
    global_rows = first_row + jnp.arange(suction_potential.shape[0], dtype=jnp.int32)
    global_cols = first_col + jnp.arange(suction_potential.shape[1], dtype=jnp.int32)
    open_rows = ((global_rows[:-1] >= 0) & (global_rows[1:] <= rows_all - 1))[:, None, None]
    open_cols = ((global_cols[:-1] >= 0) & (global_cols[1:] <= cols_all - 1))[None, :, None]
    flux_rows = jnp.where(
        open_rows,
        0.5 * (conduct[1:] + conduct[:-1]) * (suction_potential[1:] - suction_potential[:-1]),
        0.0,
    )
    flux_cols = jnp.where(
        open_cols,
        0.5
        * (conduct[:, 1:] + conduct[:, :-1])
        * (suction_potential[:, 1:] - suction_potential[:, :-1]),
        0.0,
    )
    flux_up = (
        0.5
        * (conduct[..., 1:] + conduct[..., :-1])
        * (suction_potential[..., 1:] - suction_potential[..., :-1] + 1.0)
    )
    zeros_up = jnp.zeros(suction_potential.shape[:2] + (1,), suction_potential.dtype)
    change_up = jnp.concatenate([flux_up, zeros_up], 2) - jnp.concatenate([zeros_up, flux_up], 2)
    change = (
        flux_rows[1:, 1:-1]
        - flux_rows[:-1, 1:-1]
        + (flux_cols[1:-1, 1:] - flux_cols[1:-1, :-1])
        + change_up[1:-1, 1:-1]
    )
    inside = ((global_rows[1:-1] >= 0) & (global_rows[1:-1] <= rows_all - 1))[:, None, None] & (
        (global_cols[1:-1] >= 0) & (global_cols[1:-1] <= cols_all - 1)
    )[None, :, None]
    head_new = jnp.where(inside, suction_potential[1:-1, 1:-1] + change, 0.0)
    vertical = jnp.concatenate([temp[..., 1:], zeros_up], 2) + jnp.concatenate(
        [zeros_up, temp[..., :-1]], 2
    )
    laplace = (
        temp[2:, 1:-1]
        + temp[:-2, 1:-1]
        + temp[1:-1, 2:]
        + temp[1:-1, :-2]
        + vertical[1:-1, 1:-1]
        - 6.0 * temp[1:-1, 1:-1]
    )
    temp_new = jnp.where(inside, temp[1:-1, 1:-1] + DIFFUSE * laplace, 0.0)
    return (head_new, temp_new, conduct_sat[1:-1, 1:-1], alpha[1:-1, 1:-1], ice[1:-1, 1:-1])


def moisture(suction_potential):
    return 0.05 + 0.4 * jnp.exp(0.8 * jnp.minimum(suction_potential, 0.0))


def render(theta, first_plane, planes_all, groups, tilt, gain, middle):
    depth_z = theta.shape[2]
    planes = first_plane + jnp.arange(theta.shape[1], dtype=jnp.int32)
    shift = tilt * (planes.astype(jnp.float32) - 0.5 * planes_all)
    wrapped = shift - depth_z * jnp.floor(shift / depth_z)
    base = jnp.floor(wrapped)
    frac = wrapped - base
    offset = base.astype(jnp.int32) % depth_z
    doubled = jnp.concatenate([theta, theta], 2)

    def plane_slices(column, start):
        lower_part = lax.dynamic_slice_in_dim(column, start, depth_z, 1)
        upper_part = lax.dynamic_slice_in_dim(column, start + 1, depth_z, 1)
        return (lower_part, upper_part)

    lower_vals, upper_vals = jax.vmap(plane_slices, in_axes=(1, 0), out_axes=(1, 1))(
        doubled, offset
    )
    sample = (1.0 - frac)[None, :, None] * lower_vals + frac[None, :, None] * upper_vals
    shape_four = (theta.shape[0], groups, theta.shape[1] // groups, depth_z)
    sample = sample.reshape(shape_four)
    optical = sample * (8.0 / planes_all)
    before = jnp.cumsum(optical, axis=2) - optical
    weight = (1.0 - jnp.exp(-optical)) * jnp.exp(-before)
    layers = [
        jnp.sum(jax.nn.sigmoid(gain[color] * (sample - middle[color])) * weight, axis=2)
        for color in range(3)
    ]
    layers.append(jnp.sum(optical, axis=2))
    return jnp.stack(layers, 0).transpose(2, 0, 1, 3)


def shards(
    suction_potential,
    ground_warmth,
    ground_category,
    icebound_flag,
    ground_wetted_permeability,
    ground_falloff_exponent,
    camera_skew_per_plane,
    hue_gradient_steepness,
    hue_gradient_middles,
    camera_distance_ordering,
):
    rows_dev = suction_potential.shape[0]
    cols_dev = suction_potential.shape[1]
    rows_all = rows_dev * lax.axis_size("gx")
    cols_all = cols_dev * lax.axis_size("gy")
    row_start = lax.axis_index("gx") * rows_dev
    col_start = lax.axis_index("gy") * cols_dev
    evolving_arrays = (
        suction_potential,
        ground_warmth,
        voxel_index_map(ground_category, ground_wetted_permeability),
        voxel_index_map(ground_category, ground_falloff_exponent),
        icebound_flag.astype(jnp.float32),
    )
    extended = with_halo(jnp.stack(evolving_arrays), (("gx", 1), ("gy", 2)), STEPS)
    evolving_arrays = tuple((extended[number] for number in range(5)))
    for number in range(STEPS):
        margin = STEPS - number
        evolving_arrays = advance(
            evolving_arrays, row_start - margin, col_start - margin, rows_all, cols_all
        )
    theta = moisture(evolving_arrays[0])

    def one_view(tilt):
        return render(
            theta, col_start, cols_all, 1, tilt, hue_gradient_steepness, hue_gradient_middles
        )[0]

    pieces = lax.map(one_view, camera_skew_per_plane)
    received = lax.all_to_all(pieces[None], "gy", split_axis=4, concat_axis=0, tiled=True)
    in_front = (camera_distance_ordering[:, None, :] < camera_distance_ordering[:, :, None]).astype(
        jnp.float32
    )
    depth = received[:, :, 3]
    front = jnp.einsum("vij,jvxz->ivxz", in_front, depth, precision=lax.Precision.HIGHEST)
    color = jnp.sum(jnp.exp(-front)[:, :, None] * received[:, :, :3], axis=0)
    opacity = 1.0 - jnp.exp(-jnp.sum(depth, axis=0))
    image = jnp.concatenate([color, opacity[:, None]], 1)
    return (evolving_arrays[0], evolving_arrays[1], image)


def solution(mesh):
    placed = (
        P("gx", "gy", None),
        P("gx", "gy", None),
        P("gx", "gy", None),
        P("gx", "gy", None),
        P(),
        P(),
        P(),
        P(),
        P(),
        P(),
    )
    return jax.shard_map(
        shards,
        mesh=mesh,
        in_specs=placed,
        out_specs=(P("gx", "gy", None), P("gx", "gy", None), P(None, None, "gx", "gy")),
        check_vma=False,
    )
```

profile of v0, /device:TPU:0, one launch (start us, length us, event | category | flops | bytes accessed | tf_op | source)
XLA Modules:
  0.0 95.9 jit_solution(1274984922315434157)
XLA Ops:
  0.6 1.8 %fusion.79 = (f32[1]{0:T(128)}, f32[1]{0:T(128)}, f32[1]{0:T(128)}, f32[1]{0:T(128)}, f32[1]{0:T(128)}, /*index=5*/f32[1]{0:T(128)}, f32[1]{0:T(128)}, f32[1]{0:...) fusion(f32[12]{0:T(128)} %param.16), kind=kLoop, calls=%fused_computation.171 | loop fusion | bytes 96 | tf_op jit(solution)/shard_map/slice | solution.py:27
  2.4 0.8 bitcast_dynamic-update-slice_fusion.4
  3.2 0.7 fusion.78
  3.9 0.7 copy-done.5
  4.7 7.6 %bitcast_dynamic-update-slice_fusion.2 = (f32[5,8,8,128]{3,2,1,0:T(8,128)S(1)}, pred[8,8,128]{2,1,0:T(8,128)(4,1)S(1)}, pred[8,8,128]{2,1,0:T(8,128)(4,1)S(1)}, ...) fusion(f32[5,8,8,128]{3,2,1,0:T(8,128)S(1)} %bitcast_dynamic-up, ...), kind=kLoop, calls=%fused_computation.130 | loop fusion | flops 286720 | bytes 163888
  12.3 7.6 %bitcast_dynamic-update-slice_fusion.1 = f32[5,8,8,128]{3,2,1,0:T(8,128)S(1)} fusion(f32[5,8,8,128]{3,2,1,0:T(8,128)S(1)} %get-tuple-element.160, pred[8,8,128]{2,1,0:T(8,128)(4,1)S(1)} %get-tuple-element.172, pred[8,8,128]{2,1,0:T(8,128)(4,1)S(1)} %get-tuple-element.171, pred[8,8,128]{2,1,0:T(8,128)(4,1)S(1)} %get-tuple-element.170, ...), kind=kLoop, calls=%fused_computation.129 | loop fusion | flops 188416 | bytes 131120
  19.9 2.4 %collective-permute-start = (f32[5,2,8,128]{3,2,1,0:T(8,128)S(1)}, f32[5,2,8,128]{3,2,1,0:T(8,128)S(1)}, u32[]{:S(2)}, u32[]{:S(2)}) collective-permute-start(f32[5,2,8,128]{3,2,1,0:T(8,128)S(1)} %get-tuple-element.191), channel_id=1, source_target_pairs={{0,4},{4,8},{8,12},{12,16},{16,20},{20,24},{24,28},{1,5},{5,9},{9,... | collective-permute-start | bytes 122888 | tf_op jit(solution)/shard_map/ppermute | solution.py:18
  22.3 1.3 %collective-permute-start.1 = (f32[5,2,8,128]{3,2,1,0:T(8,128)S(1)}, f32[5,2,8,128]{3,2,1,0:T(8,128)S(1)}, u32[]{:S(2)}, u32[]{:S(2)}) collective-permute-start(f32[5,2,8,128]{3,2,1,0:T(8,128)S(1)} %get-tuple-element.192), channel_id=1, source_target_pairs={{4,0},{8,4},{12,8},{16,12},{20,16},{24,20},{28,24},{5,1},{9,5},{13... | collective-permute-start | bytes 122888 | tf_op jit(solution)/shard_map/ppermute | solution.py:19
  24.2 3.4 %collective-permute-done.1 = f32[5,2,8,128]{3,2,1,0:T(8,128)S(1)} collective-permute-done((f32[5,2,8,128]{3,2,1,0:T(8,128)S(1)}, f32[5,2,8,128]{3,2,1,0:T(8,128)S(1)}, u32[]{:S(2)}, u32[]{:S(2)}) %collective-permute-start.1) | collective-permute-done | bytes 40992 | tf_op jit(solution)/shard_map/ppermute | solution.py:19
  27.7 3.4 %collective-permute-start.2 = (f32[5,12,2,128]{3,2,1,0:T(2,128)S(1)}, f32[5,12,2,128]{3,2,1,0:T(2,128)S(1)}, u32[]{:S(2)}, u32[]{:S(2)}) collective-permute-start(f32[5,12,2,128]{3,2,1,0:T(2,128)S(1)} %get-tuple-element.189), channel_id=1, source_target_pairs={{0,1},{1,2},{2,3},{4,5},{5,6},{6,7},{8,9},{9,10},{10,11},{12,13},{... | collective-permute-start | bytes 184328 | tf_op jit(solution)/shard_map/ppermute | solution.py:18
  31.1 1.3 %collective-permute-start.3 = (f32[5,12,2,128]{3,2,1,0:T(2,128)S(1)}, f32[5,12,2,128]{3,2,1,0:T(2,128)S(1)}, u32[]{:S(2)}, u32[]{:S(2)}) collective-permute-start(f32[5,12,2,128]{3,2,1,0:T(2,128)S(1)} %get-tuple-element.190), channel_id=1, source_target_pairs={{1,0},{2,1},{3,2},{5,4},{6,5},{7,6},{9,8},{10,9},{11,10},{13,12},{... | collective-permute-start | bytes 184328 | tf_op jit(solution)/shard_map/ppermute | solution.py:19
  32.9 4.3 %collective-permute-done.3 = f32[5,12,2,128]{3,2,1,0:T(2,128)S(1)} collective-permute-done((f32[5,12,2,128]{3,2,1,0:T(2,128)S(1)}, f32[5,12,2,128]{3,2,1,0:T(2,128)S(1)}, u32[]{:S(2)}, u32[]{:S(2)}) %collective-permute-start.3) | collective-permute-done | bytes 61472 | tf_op jit(solution)/shard_map/ppermute | solution.py:19
  38.3 0.7 multiply_add_fusion.1
  39.8 40.9 %while.12 = (s32[]{:T(128)}, f32[4,4,8,128]{3,2,1,0:T(8,128)S(1)}, f32[3]{0:T(128)S(1)}, f32[4]{0:T(128)S(1)}, s32[]{:T(128)}, /*index=5*/f32[8,8,256]{0,1,2:T(8,128)S(1)}, f32[3]{0:T(128)S(1)}, s32[]{:T(128)}) while((s32[]{:T(128)}, f32[4,4,8,128]{3,2,1,0:T(8,128)S(1)}, f32[3]{0:T(128)S(1)}, f32[4]{0:T(128)S(1)}, s32[]{:T(128)}, ...), condition=%wide.region_6.7_spmd, body=%wide.region_0.6_spmd.sunk | while | flops 352634 | bytes 442941 | solution.py:161
  41.0 1.3 %gather_fusion = f32[8,8,128]{1,0,2:T(8,128)S(1)} fusion(f32[8,8,256]{1,0,2:T(8,128)S(1)} %bitcast.158, s32[8]{0:T(128)S(1)} %get-tuple-element.290), kind=kCustom, calls=%fused_computation.1.clone.1 | custom fusion | bytes 65632 | tf_op jit(solution)/shard_map/while/body/eval_jaxpr/vmap()/gather | solution.py:102
  42.6 1.3 %gather_fusion.1 = f32[8,8,128]{1,0,2:T(8,128)S(1)} fusion(f32[8,8,256]{1,0,2:T(8,128)S(1)} %bitcast.159, s32[8]{0:T(128)S(1)} %get-tuple-element.292), kind=kCustom, calls=%fused_computation.clone.1 | custom fusion | bytes 65632 | tf_op jit(solution)/shard_map/while/body/eval_jaxpr/vmap()/gather | solution.py:101
  44.1 0.7 fusion.83
  45.4 3.9 %fusion.84 = (f32[8,128]{1,0:T(8,128)S(1)}, f32[8,128]{1,0:T(8,128)S(1)}, f32[8,128]{1,0:T(8,128)S(1)}, f32[8,128]{1,0:T(8,128)S(1)}) fusion(f32[]{:T(128)} %bitcast.146, f32[]{:T(128)} %bitcast.147, f32[]{:T(128)} %bitcast.148, f32[]{:T(128)} %bitcast.149, f32[]{:T(128)} %bitcast.150, f32[]{:T(128)} %bitcast.151, f32[8,8,128]{2,1,0:T(8,128)S(1)} %copy.67, ...), kind=kOutput, calls=%fused_computation.16.clone.1 | output fusion | flops 339968 | bytes 82008 | tf_op jit(solution)/shard_map/while/body/eval_jaxpr/jit(cumsum)/reduce_window_sum | solution.py:112
  51.3 1.3 %gather_fusion = f32[8,8,128]{1,0,2:T(8,128)S(1)} fusion(f32[8,8,256]{1,0,2:T(8,128)S(1)} %bitcast.158, s32[8]{0:T(128)S(1)} %get-tuple-element.290), kind=kCustom, calls=%fused_computation.1.clone.1 | custom fusion | bytes 65632 | tf_op jit(solution)/shard_map/while/body/eval_jaxpr/vmap()/gather | solution.py:102
  52.8 1.3 %gather_fusion.1 = f32[8,8,128]{1,0,2:T(8,128)S(1)} fusion(f32[8,8,256]{1,0,2:T(8,128)S(1)} %bitcast.159, s32[8]{0:T(128)S(1)} %get-tuple-element.292), kind=kCustom, calls=%fused_computation.clone.1 | custom fusion | bytes 65632 | tf_op jit(solution)/shard_map/while/body/eval_jaxpr/vmap()/gather | solution.py:101
  54.3 0.7 fusion.83
  55.6 3.9 %fusion.84 = (f32[8,128]{1,0:T(8,128)S(1)}, f32[8,128]{1,0:T(8,128)S(1)}, f32[8,128]{1,0:T(8,128)S(1)}, f32[8,128]{1,0:T(8,128)S(1)}) fusion(f32[]{:T(128)} %bitcast.146, f32[]{:T(128)} %bitcast.147, f32[]{:T(128)} %bitcast.148, f32[]{:T(128)} %bitcast.149, f32[]{:T(128)} %bitcast.150, f32[]{:T(128)} %bitcast.151, f32[8,8,128]{2,1,0:T(8,128)S(1)} %copy.67, ...), kind=kOutput, calls=%fused_computation.16.clone.1 | output fusion | flops 339968 | bytes 82008 | tf_op jit(solution)/shard_map/while/body/eval_jaxpr/jit(cumsum)/reduce_window_sum | solution.py:112
  61.5 1.3 %gather_fusion = f32[8,8,128]{1,0,2:T(8,128)S(1)} fusion(f32[8,8,256]{1,0,2:T(8,128)S(1)} %bitcast.158, s32[8]{0:T(128)S(1)} %get-tuple-element.290), kind=kCustom, calls=%fused_computation.1.clone.1 | custom fusion | bytes 65632 | tf_op jit(solution)/shard_map/while/body/eval_jaxpr/vmap()/gather | solution.py:102
  63.0 1.3 %gather_fusion.1 = f32[8,8,128]{1,0,2:T(8,128)S(1)} fusion(f32[8,8,256]{1,0,2:T(8,128)S(1)} %bitcast.159, s32[8]{0:T(128)S(1)} %get-tuple-element.292), kind=kCustom, calls=%fused_computation.clone.1 | custom fusion | bytes 65632 | tf_op jit(solution)/shard_map/while/body/eval_jaxpr/vmap()/gather | solution.py:101
  65.9 3.9 %fusion.84 = (f32[8,128]{1,0:T(8,128)S(1)}, f32[8,128]{1,0:T(8,128)S(1)}, f32[8,128]{1,0:T(8,128)S(1)}, f32[8,128]{1,0:T(8,128)S(1)}) fusion(f32[]{:T(128)} %bitcast.146, f32[]{:T(128)} %bitcast.147, f32[]{:T(128)} %bitcast.148, f32[]{:T(128)} %bitcast.149, f32[]{:T(128)} %bitcast.150, f32[]{:T(128)} %bitcast.151, f32[8,8,128]{2,1,0:T(8,128)S(1)} %copy.67, ...), kind=kOutput, calls=%fused_computation.16.clone.1 | output fusion | flops 339968 | bytes 82008 | tf_op jit(solution)/shard_map/while/body/eval_jaxpr/jit(cumsum)/reduce_window_sum | solution.py:112
  71.7 1.3 %gather_fusion = f32[8,8,128]{1,0,2:T(8,128)S(1)} fusion(f32[8,8,256]{1,0,2:T(8,128)S(1)} %bitcast.158, s32[8]{0:T(128)S(1)} %get-tuple-element.290), kind=kCustom, calls=%fused_computation.1.clone.1 | custom fusion | bytes 65632 | tf_op jit(solution)/shard_map/while/body/eval_jaxpr/vmap()/gather | solution.py:102
  73.2 1.3 %gather_fusion.1 = f32[8,8,128]{1,0,2:T(8,128)S(1)} fusion(f32[8,8,256]{1,0,2:T(8,128)S(1)} %bitcast.159, s32[8]{0:T(128)S(1)} %get-tuple-element.292), kind=kCustom, calls=%fused_computation.clone.1 | custom fusion | bytes 65632 | tf_op jit(solution)/shard_map/while/body/eval_jaxpr/vmap()/gather | solution.py:101
  76.1 3.9 %fusion.84 = (f32[8,128]{1,0:T(8,128)S(1)}, f32[8,128]{1,0:T(8,128)S(1)}, f32[8,128]{1,0:T(8,128)S(1)}, f32[8,128]{1,0:T(8,128)S(1)}) fusion(f32[]{:T(128)} %bitcast.146, f32[]{:T(128)} %bitcast.147, f32[]{:T(128)} %bitcast.148, f32[]{:T(128)} %bitcast.149, f32[]{:T(128)} %bitcast.150, f32[]{:T(128)} %bitcast.151, f32[8,8,128]{2,1,0:T(8,128)S(1)} %copy.67, ...), kind=kOutput, calls=%fused_computation.16.clone.1 | output fusion | flops 339968 | bytes 82008 | tf_op jit(solution)/shard_map/while/body/eval_jaxpr/jit(cumsum)/reduce_window_sum | solution.py:112
  81.3 1.1 %reshape.252 = f32[4,1,4096]{2,1,0:T(1,128)S(1)} reshape(f32[128,1,4,4,8]{4,3,2,1,0:T(4,128)S(1)} %bitcast_bitcast_fusion) | data formatting | bytes 131072
  82.5 8.5 %all_to_all.18 = f32[4,1,4096]{2,1,0:T(1,128)S(1)} all-to-all(f32[4,1,4096]{2,1,0:T(1,128)S(1)} %reshape.252), channel_id=1, replica_groups=mesh['gx'=8,'gy'=4] {'gy'}, dimensions={0} | all-to-all | bytes 131072 | tf_op jit(solution)/shard_map/all_to_all | solution.py:162
  91.5 0.8 reduce.21
  92.3 1.3 %reshape.253 = f32[128,1,4,4,8]{4,3,2,1,0:T(4,128)S(1)} reshape(f32[4,4096]{1,0:T(4,128)S(1)} %reduce.21) | data formatting | bytes 131072
  (115 shorter events, 19.7 us)
Async XLA Ops:
  2.4 0.8 copy-start.2
  2.4 1.5 %copy-start.3 = (f32[8,8,128]{2,1,0:T(8,128)S(1)}, f32[8,8,128]{2,1,0:T(8,128)}, u32[]{:S(2)}) copy-start(f32[8,8,128]{2,1,0:T(8,128)} %param.13) | copy-start | bytes 98308
  3.9 0.8 copy-start.5
  12.3 7.6 %copy-start.4 = (s32[8,8,128]{2,1,0:T(8,128)S(1)}, s32[8,8,128]{2,1,0:T(8,128)}, u32[]{:S(2)}) copy-start(s32[8,8,128]{2,1,0:T(8,128)} %param.15) | copy-start | bytes 98308
  19.9 4.3 %collective-permute-start = (f32[5,2,8,128]{3,2,1,0:T(8,128)S(1)}, f32[5,2,8,128]{3,2,1,0:T(8,128)S(1)}, u32[]{:S(2)}, u32[]{:S(2)}) collective-permute-start(f32[5,2,8,128]{3,2,1,0:T(8,128)S(1)} %get-tuple-element.191), channel_id=1, source_target_pairs={{0,4},{4,8},{8,12},{12,16},{16,20},{20,24},{24,28},{1,5},{5,9},{9,... | collective-permute-start | bytes 122888 | tf_op jit(solution)/shard_map/ppermute | solution.py:18
  22.3 5.3 %collective-permute-start.1 = (f32[5,2,8,128]{3,2,1,0:T(8,128)S(1)}, f32[5,2,8,128]{3,2,1,0:T(8,128)S(1)}, u32[]{:S(2)}, u32[]{:S(2)}) collective-permute-start(f32[5,2,8,128]{3,2,1,0:T(8,128)S(1)} %get-tuple-element.192), channel_id=1, source_target_pairs={{4,0},{8,4},{12,8},{16,12},{20,16},{24,20},{28,24},{5,1},{9,5},{13... | collective-permute-start | bytes 122888 | tf_op jit(solution)/shard_map/ppermute | solution.py:19
  27.7 5.3 %collective-permute-start.2 = (f32[5,12,2,128]{3,2,1,0:T(2,128)S(1)}, f32[5,12,2,128]{3,2,1,0:T(2,128)S(1)}, u32[]{:S(2)}, u32[]{:S(2)}) collective-permute-start(f32[5,12,2,128]{3,2,1,0:T(2,128)S(1)} %get-tuple-element.189), channel_id=1, source_target_pairs={{0,1},{1,2},{2,3},{4,5},{5,6},{6,7},{8,9},{9,10},{10,11},{12,13},{... | collective-permute-start | bytes 184328 | tf_op jit(solution)/shard_map/ppermute | solution.py:18
  31.1 6.1 %collective-permute-start.3 = (f32[5,12,2,128]{3,2,1,0:T(2,128)S(1)}, f32[5,12,2,128]{3,2,1,0:T(2,128)S(1)}, u32[]{:S(2)}, u32[]{:S(2)}) collective-permute-start(f32[5,12,2,128]{3,2,1,0:T(2,128)S(1)} %get-tuple-element.190), channel_id=1, source_target_pairs={{1,0},{2,1},{3,2},{5,4},{6,5},{7,6},{9,8},{10,9},{11,10},{13,12},{... | collective-permute-start | bytes 184328 | tf_op jit(solution)/shard_map/ppermute | solution.py:19
  39.1 0.7 copy-start
  39.1 0.7 copy-start.1
  39.1 0.7 copy-start.7
  94.2 0.7 copy-start.6
where the time goes:
time: 96.9 us; the launch traced here: 95.9 us
  other arithmetic  39.2 us (40%)
  local copies, waits for them, and re-layouts  30.4 us (31%)
  blocking collectives  8.45 us (9%)
  starting transfers between devices  8.38 us (9%)
  waiting for transfers between devices  8.16 us (8%)
    another operation x4, other arithmetic, render(): before = jnp.cumsum(optical, axis=2) - optical  15.5 us
    unnamed x2, other arithmetic  15.2 us
    all_to_all x1, blocking collectives, shards(): lax.all_to_all(pieces[None], 'gy', split_axis=4, concat_axis=0, tiled=True)  8.45 us
    ppermute x2, waiting for transfers between devices, with_halo(): after = lax.ppermute(first, axis, down)  7.69 us
    gather x8, local copies, waits for them, and re-layouts, plane_slices(): lower_part = lax.dynamic_slice_in_dim(column, start, depth_z, 1)  6.08 us
    gather x8, local copies, waits for them, and re-layouts, plane_slices(): upper_part = lax.dynamic_slice_in_dim(column, start + 1, depth_z, 1)  6 us
    ppermute x2, starting transfers between devices, with_halo(): before = lax.ppermute(last, axis, up)  5.8 us
    unnamed x22, local copies, waits for them, and re-layouts  5.52 us
  transfers between devices with their start and end apart: 4, of which 3 were waited for; matrix products, arithmetic and copies ran while one was open for 1% of the time, Pallas kernels for 0%

commit v1 on v0

--- a/solution.py
+++ b/solution.py
@@ -2,6 +2,7 @@
 import jax.numpy as jnp
 from jax import lax
 from jax.sharding import PartitionSpec as P
+from jax.lax import all_to_all, psum
 
 STEPS = 2
 IMPEDANCE = 4.0
@@ -159,7 +160,13 @@
         )[0]
 
     pieces = lax.map(one_view, camera_skew_per_plane)
-    received = lax.all_to_all(pieces[None], "gy", split_axis=4, concat_axis=0, tiled=True)
+    unit = pieces[None]
+    received = jnp.concatenate(
+        all_to_all(
+            jnp.stack(jnp.split(unit, psum(1, "gy"), 4), axis=0), "gy", split_axis=0, concat_axis=0
+        ),
+        0,
+    )
     in_front = (camera_distance_ordering[:, None, :] < camera_distance_ordering[:, :, None]).astype(
         jnp.float32
     )

time: 96.9 us -> 94.1 us (0.971)
  local copies, waits for them, and re-layouts: 30.4 us -> 27.1 us
    unnamed x22 -> x21, local copies, waits for them, and re-layouts: 5.52 us -> 3.34 us
    unnamed x2 -> x3, other arithmetic: 15.2 us -> 15.2 us
where the time goes in v1:
time: 94.1 us; the launch traced here: 93.1 us
  other arithmetic  39.6 us (42%)
  local copies, waits for them, and re-layouts  27.1 us (29%)
  blocking collectives  8.45 us (9%)
  starting transfers between devices  8.38 us (9%)
  waiting for transfers between devices  8.16 us (9%)
    another operation x4, other arithmetic, render(): before = jnp.cumsum(optical, axis=2) - optical  15.7 us
    unnamed x3, other arithmetic  15.2 us
    all_to_all x1, blocking collectives, shards(): all_to_all(jnp.stack(jnp.split(unit, psum(1, 'gy'), 4), axis=0), 'gy', sp...  8.45 us
    ppermute x2, waiting for transfers between devices, with_halo(): after = lax.ppermute(first, axis, down)  7.69 us
    gather x8, local copies, waits for them, and re-layouts, plane_slices(): lower_part = lax.dynamic_slice_in_dim(column, start, depth_z, 1)  6.08 us
    gather x8, local copies, waits for them, and re-layouts, plane_slices(): upper_part = lax.dynamic_slice_in_dim(column, start + 1, depth_z, 1)  6 us
    ppermute x2, starting transfers between devices, with_halo(): before = lax.ppermute(last, axis, up)  5.8 us
    unnamed x21, local copies, waits for them, and re-layouts  3.34 us
  transfers between devices with their start and end apart: 4, of which 3 were waited for; matrix products, arithmetic and copies ran while one was open for 1% of the time, Pallas kernels for 0%

profile of v1, /device:TPU:0, one launch (start us, length us, event | category | flops | bytes accessed | tf_op | source)
XLA Modules:
  0.0 93.1 jit_solution(7099288206636146126)
XLA Ops:
  0.6 1.8 %fusion.79 = (f32[1]{0:T(128)}, f32[1]{0:T(128)}, f32[1]{0:T(128)}, f32[1]{0:T(128)}, f32[1]{0:T(128)}, /*index=5*/f32[1]{0:T(128)}, f32[1]{0:T(128)}, f32[1]{0:...) fusion(f32[12]{0:T(128)} %param.16), kind=kLoop, calls=%fused_computation.177 | loop fusion | bytes 96 | tf_op jit(solution)/shard_map/slice | solution.py:28
  2.4 0.8 bitcast_dynamic-update-slice_fusion.4
  3.2 0.7 fusion.78
  3.9 0.7 copy-done.5
  4.7 7.6 %bitcast_dynamic-update-slice_fusion.2 = (f32[5,8,8,128]{3,2,1,0:T(8,128)S(1)}, pred[8,8,128]{2,1,0:T(8,128)(4,1)S(1)}, pred[8,8,128]{2,1,0:T(8,128)(4,1)S(1)}, ...) fusion(f32[5,8,8,128]{3,2,1,0:T(8,128)S(1)} %bitcast_dynamic-up, ...), kind=kLoop, calls=%fused_computation.136 | loop fusion | flops 286720 | bytes 163888
  12.3 7.5 %bitcast_dynamic-update-slice_fusion.1 = f32[5,8,8,128]{3,2,1,0:T(8,128)S(1)} fusion(f32[5,8,8,128]{3,2,1,0:T(8,128)S(1)} %get-tuple-element.160, pred[8,8,128]{2,1,0:T(8,128)(4,1)S(1)} %get-tuple-element.172, pred[8,8,128]{2,1,0:T(8,128)(4,1)S(1)} %get-tuple-element.171, pred[8,8,128]{2,1,0:T(8,128)(4,1)S(1)} %get-tuple-element.170, ...), kind=kLoop, calls=%fused_computation.135 | loop fusion | flops 188416 | bytes 131120
  19.9 2.4 %collective-permute-start = (f32[5,2,8,128]{3,2,1,0:T(8,128)S(1)}, f32[5,2,8,128]{3,2,1,0:T(8,128)S(1)}, u32[]{:S(2)}, u32[]{:S(2)}) collective-permute-start(f32[5,2,8,128]{3,2,1,0:T(8,128)S(1)} %get-tuple-element.191), channel_id=1, source_target_pairs={{0,4},{4,8},{8,12},{12,16},{16,20},{20,24},{24,28},{1,5},{5,9},{9,... | collective-permute-start | bytes 122888 | tf_op jit(solution)/shard_map/ppermute | solution.py:19
  22.3 1.3 %collective-permute-start.1 = (f32[5,2,8,128]{3,2,1,0:T(8,128)S(1)}, f32[5,2,8,128]{3,2,1,0:T(8,128)S(1)}, u32[]{:S(2)}, u32[]{:S(2)}) collective-permute-start(f32[5,2,8,128]{3,2,1,0:T(8,128)S(1)} %get-tuple-element.192), channel_id=1, source_target_pairs={{4,0},{8,4},{12,8},{16,12},{20,16},{24,20},{28,24},{5,1},{9,5},{13... | collective-permute-start | bytes 122888 | tf_op jit(solution)/shard_map/ppermute | solution.py:20
  24.2 3.4 %collective-permute-done.1 = f32[5,2,8,128]{3,2,1,0:T(8,128)S(1)} collective-permute-done((f32[5,2,8,128]{3,2,1,0:T(8,128)S(1)}, f32[5,2,8,128]{3,2,1,0:T(8,128)S(1)}, u32[]{:S(2)}, u32[]{:S(2)}) %collective-permute-start.1) | collective-permute-done | bytes 40992 | tf_op jit(solution)/shard_map/ppermute | solution.py:20
  27.7 3.4 %collective-permute-start.2 = (f32[5,12,2,128]{3,2,1,0:T(2,128)S(1)}, f32[5,12,2,128]{3,2,1,0:T(2,128)S(1)}, u32[]{:S(2)}, u32[]{:S(2)}) collective-permute-start(f32[5,12,2,128]{3,2,1,0:T(2,128)S(1)} %get-tuple-element.189), channel_id=1, source_target_pairs={{0,1},{1,2},{2,3},{4,5},{5,6},{6,7},{8,9},{9,10},{10,11},{12,13},{... | collective-permute-start | bytes 184328 | tf_op jit(solution)/shard_map/ppermute | solution.py:19
  31.1 1.3 %collective-permute-start.3 = (f32[5,12,2,128]{3,2,1,0:T(2,128)S(1)}, f32[5,12,2,128]{3,2,1,0:T(2,128)S(1)}, u32[]{:S(2)}, u32[]{:S(2)}) collective-permute-start(f32[5,12,2,128]{3,2,1,0:T(2,128)S(1)} %get-tuple-element.190), channel_id=1, source_target_pairs={{1,0},{2,1},{3,2},{5,4},{6,5},{7,6},{9,8},{10,9},{11,10},{13,12},{... | collective-permute-start | bytes 184328 | tf_op jit(solution)/shard_map/ppermute | solution.py:20
  32.9 4.3 %collective-permute-done.3 = f32[5,12,2,128]{3,2,1,0:T(2,128)S(1)} collective-permute-done((f32[5,12,2,128]{3,2,1,0:T(2,128)S(1)}, f32[5,12,2,128]{3,2,1,0:T(2,128)S(1)}, u32[]{:S(2)}, u32[]{:S(2)}) %collective-permute-start.3) | collective-permute-done | bytes 61472 | tf_op jit(solution)/shard_map/ppermute | solution.py:20
  38.3 0.7 multiply_add_fusion.1
  39.8 41.1 %while.12 = (s32[]{:T(128)}, f32[4,4,8,128]{3,2,0,1:T(8,128)S(1)}, f32[3]{0:T(128)S(1)}, f32[4]{0:T(128)S(1)}, s32[]{:T(128)}, /*index=5*/f32[8,8,256]{0,1,2:T(8,128)S(1)}, f32[3]{0:T(128)S(1)}, s32[]{:T(128)}) while((s32[]{:T(128)}, f32[4,4,8,128]{3,2,0,1:T(8,128)S(1)}, f32[3]{0:T(128)S(1)}, f32[4]{0:T(128)S(1)}, s32[]{:T(128)}, ...), condition=%wide.region_6.7_spmd, body=%wide.region_0.6_spmd.sunk | while | flops 352634 | bytes 442941 | solution.py:162
  41.0 1.3 %gather_fusion = f32[8,8,128]{1,0,2:T(8,128)S(1)} fusion(f32[8,8,256]{1,0,2:T(8,128)S(1)} %bitcast.166, s32[8]{0:T(128)S(1)} %get-tuple-element.294), kind=kCustom, calls=%fused_computation.1.clone.1 | custom fusion | bytes 65632 | tf_op jit(solution)/shard_map/while/body/eval_jaxpr/vmap()/gather | solution.py:103
  42.5 1.3 %gather_fusion.1 = f32[8,8,128]{1,0,2:T(8,128)S(1)} fusion(f32[8,8,256]{1,0,2:T(8,128)S(1)} %bitcast.167, s32[8]{0:T(128)S(1)} %get-tuple-element.296), kind=kCustom, calls=%fused_computation.clone.1 | custom fusion | bytes 65632 | tf_op jit(solution)/shard_map/while/body/eval_jaxpr/vmap()/gather | solution.py:102
  44.1 0.7 fusion.84
  45.4 3.9 %fusion.85 = (f32[8,128]{1,0:T(8,128)S(1)}, f32[8,128]{1,0:T(8,128)S(1)}, f32[8,128]{1,0:T(8,128)S(1)}, f32[8,128]{1,0:T(8,128)S(1)}) fusion(f32[]{:T(128)} %bitcast.154, f32[]{:T(128)} %bitcast.155, f32[]{:T(128)} %bitcast.156, f32[]{:T(128)} %bitcast.157, f32[]{:T(128)} %bitcast.158, f32[]{:T(128)} %bitcast.159, f32[8,8,128]{2,1,0:T(8,128)S(1)} %copy.83, ...), kind=kOutput, calls=%fused_computation.16.clone.1 | output fusion | flops 339968 | bytes 82008 | tf_op jit(solution)/shard_map/while/body/eval_jaxpr/jit(cumsum)/reduce_window_sum | solution.py:113
  51.3 1.3 %gather_fusion = f32[8,8,128]{1,0,2:T(8,128)S(1)} fusion(f32[8,8,256]{1,0,2:T(8,128)S(1)} %bitcast.166, s32[8]{0:T(128)S(1)} %get-tuple-element.294), kind=kCustom, calls=%fused_computation.1.clone.1 | custom fusion | bytes 65632 | tf_op jit(solution)/shard_map/while/body/eval_jaxpr/vmap()/gather | solution.py:103
  52.8 1.3 %gather_fusion.1 = f32[8,8,128]{1,0,2:T(8,128)S(1)} fusion(f32[8,8,256]{1,0,2:T(8,128)S(1)} %bitcast.167, s32[8]{0:T(128)S(1)} %get-tuple-element.296), kind=kCustom, calls=%fused_computation.clone.1 | custom fusion | bytes 65632 | tf_op jit(solution)/shard_map/while/body/eval_jaxpr/vmap()/gather | solution.py:102
  54.3 0.7 fusion.84
  55.7 3.9 %fusion.85 = (f32[8,128]{1,0:T(8,128)S(1)}, f32[8,128]{1,0:T(8,128)S(1)}, f32[8,128]{1,0:T(8,128)S(1)}, f32[8,128]{1,0:T(8,128)S(1)}) fusion(f32[]{:T(128)} %bitcast.154, f32[]{:T(128)} %bitcast.155, f32[]{:T(128)} %bitcast.156, f32[]{:T(128)} %bitcast.157, f32[]{:T(128)} %bitcast.158, f32[]{:T(128)} %bitcast.159, f32[8,8,128]{2,1,0:T(8,128)S(1)} %copy.83, ...), kind=kOutput, calls=%fused_computation.16.clone.1 | output fusion | flops 339968 | bytes 82008 | tf_op jit(solution)/shard_map/while/body/eval_jaxpr/jit(cumsum)/reduce_window_sum | solution.py:113
  61.6 1.3 %gather_fusion = f32[8,8,128]{1,0,2:T(8,128)S(1)} fusion(f32[8,8,256]{1,0,2:T(8,128)S(1)} %bitcast.166, s32[8]{0:T(128)S(1)} %get-tuple-element.294), kind=kCustom, calls=%fused_computation.1.clone.1 | custom fusion | bytes 65632 | tf_op jit(solution)/shard_map/while/body/eval_jaxpr/vmap()/gather | solution.py:103
  63.1 1.3 %gather_fusion.1 = f32[8,8,128]{1,0,2:T(8,128)S(1)} fusion(f32[8,8,256]{1,0,2:T(8,128)S(1)} %bitcast.167, s32[8]{0:T(128)S(1)} %get-tuple-element.296), kind=kCustom, calls=%fused_computation.clone.1 | custom fusion | bytes 65632 | tf_op jit(solution)/shard_map/while/body/eval_jaxpr/vmap()/gather | solution.py:102
  64.6 0.7 fusion.84
  66.0 3.9 %fusion.85 = (f32[8,128]{1,0:T(8,128)S(1)}, f32[8,128]{1,0:T(8,128)S(1)}, f32[8,128]{1,0:T(8,128)S(1)}, f32[8,128]{1,0:T(8,128)S(1)}) fusion(f32[]{:T(128)} %bitcast.154, f32[]{:T(128)} %bitcast.155, f32[]{:T(128)} %bitcast.156, f32[]{:T(128)} %bitcast.157, f32[]{:T(128)} %bitcast.158, f32[]{:T(128)} %bitcast.159, f32[8,8,128]{2,1,0:T(8,128)S(1)} %copy.83, ...), kind=kOutput, calls=%fused_computation.16.clone.1 | output fusion | flops 339968 | bytes 82008 | tf_op jit(solution)/shard_map/while/body/eval_jaxpr/jit(cumsum)/reduce_window_sum | solution.py:113
  71.9 1.3 %gather_fusion = f32[8,8,128]{1,0,2:T(8,128)S(1)} fusion(f32[8,8,256]{1,0,2:T(8,128)S(1)} %bitcast.166, s32[8]{0:T(128)S(1)} %get-tuple-element.294), kind=kCustom, calls=%fused_computation.1.clone.1 | custom fusion | bytes 65632 | tf_op jit(solution)/shard_map/while/body/eval_jaxpr/vmap()/gather | solution.py:103
  73.4 1.3 %gather_fusion.1 = f32[8,8,128]{1,0,2:T(8,128)S(1)} fusion(f32[8,8,256]{1,0,2:T(8,128)S(1)} %bitcast.167, s32[8]{0:T(128)S(1)} %get-tuple-element.296), kind=kCustom, calls=%fused_computation.clone.1 | custom fusion | bytes 65632 | tf_op jit(solution)/shard_map/while/body/eval_jaxpr/vmap()/gather | solution.py:102
  74.9 0.7 fusion.84
  76.3 3.9 %fusion.85 = (f32[8,128]{1,0:T(8,128)S(1)}, f32[8,128]{1,0:T(8,128)S(1)}, f32[8,128]{1,0:T(8,128)S(1)}, f32[8,128]{1,0:T(8,128)S(1)}) fusion(f32[]{:T(128)} %bitcast.154, f32[]{:T(128)} %bitcast.155, f32[]{:T(128)} %bitcast.156, f32[]{:T(128)} %bitcast.157, f32[]{:T(128)} %bitcast.158, f32[]{:T(128)} %bitcast.159, f32[8,8,128]{2,1,0:T(8,128)S(1)} %copy.83, ...), kind=kOutput, calls=%fused_computation.16.clone.1 | output fusion | flops 339968 | bytes 82008 | tf_op jit(solution)/shard_map/while/body/eval_jaxpr/jit(cumsum)/reduce_window_sum | solution.py:113
  81.2 8.5 %all_to_all.5 = f32[4,1,4096]{2,1,0:T(1,128)S(1)} all-to-all(f32[4,1,4096]{2,1,0:T(1,128)S(1)} %reshape.256), channel_id=1, replica_groups=mesh['gx'=8,'gy'=4] {'gy'}, dimensions={0} | all-to-all | bytes 131072 | tf_op jit(solution)/shard_map/all_to_all | solution.py:165
  90.2 0.8 reduce.21
  (115 shorter events, 17.5 us)
Async XLA Ops:
  2.4 0.8 copy-start.2
  2.4 1.5 %copy-start.3 = (f32[8,8,128]{2,1,0:T(8,128)S(1)}, f32[8,8,128]{2,1,0:T(8,128)}, u32[]{:S(2)}) copy-start(f32[8,8,128]{2,1,0:T(8,128)} %param.13) | copy-start | bytes 98308
  3.9 0.8 copy-start.5
  12.3 7.6 %copy-start.4 = (s32[8,8,128]{2,1,0:T(8,128)S(1)}, s32[8,8,128]{2,1,0:T(8,128)}, u32[]{:S(2)}) copy-start(s32[8,8,128]{2,1,0:T(8,128)} %param.15) | copy-start | bytes 98308
  19.9 4.3 %collective-permute-start = (f32[5,2,8,128]{3,2,1,0:T(8,128)S(1)}, f32[5,2,8,128]{3,2,1,0:T(8,128)S(1)}, u32[]{:S(2)}, u32[]{:S(2)}) collective-permute-start(f32[5,2,8,128]{3,2,1,0:T(8,128)S(1)} %get-tuple-element.191), channel_id=1, source_target_pairs={{0,4},{4,8},{8,12},{12,16},{16,20},{20,24},{24,28},{1,5},{5,9},{9,... | collective-permute-start | bytes 122888 | tf_op jit(solution)/shard_map/ppermute | solution.py:19
  22.3 5.3 %collective-permute-start.1 = (f32[5,2,8,128]{3,2,1,0:T(8,128)S(1)}, f32[5,2,8,128]{3,2,1,0:T(8,128)S(1)}, u32[]{:S(2)}, u32[]{:S(2)}) collective-permute-start(f32[5,2,8,128]{3,2,1,0:T(8,128)S(1)} %get-tuple-element.192), channel_id=1, source_target_pairs={{4,0},{8,4},{12,8},{16,12},{20,16},{24,20},{28,24},{5,1},{9,5},{13... | collective-permute-start | bytes 122888 | tf_op jit(solution)/shard_map/ppermute | solution.py:20
  27.7 5.3 %collective-permute-start.2 = (f32[5,12,2,128]{3,2,1,0:T(2,128)S(1)}, f32[5,12,2,128]{3,2,1,0:T(2,128)S(1)}, u32[]{:S(2)}, u32[]{:S(2)}) collective-permute-start(f32[5,12,2,128]{3,2,1,0:T(2,128)S(1)} %get-tuple-element.189), channel_id=1, source_target_pairs={{0,1},{1,2},{2,3},{4,5},{5,6},{6,7},{8,9},{9,10},{10,11},{12,13},{... | collective-permute-start | bytes 184328 | tf_op jit(solution)/shard_map/ppermute | solution.py:19
  31.1 6.1 %collective-permute-start.3 = (f32[5,12,2,128]{3,2,1,0:T(2,128)S(1)}, f32[5,12,2,128]{3,2,1,0:T(2,128)S(1)}, u32[]{:S(2)}, u32[]{:S(2)}) collective-permute-start(f32[5,12,2,128]{3,2,1,0:T(2,128)S(1)} %get-tuple-element.190), channel_id=1, source_target_pairs={{1,0},{2,1},{3,2},{5,4},{6,5},{7,6},{9,8},{10,9},{11,10},{13,12},{... | collective-permute-start | bytes 184328 | tf_op jit(solution)/shard_map/ppermute | solution.py:20
  39.1 0.7 copy-start
  39.1 0.7 copy-start.1
  39.1 0.7 copy-start.7
  91.3 0.7 copy-start.6
